TPU v7x, 32 devices: a whole 2x2x4 slice. The times are simulated.
32 devices in a mesh: energy: 8 (over y, x, core), elem: 4 (over z).
Axes of the slice: x: 2, y: 2, z: 4, core: 2. Of those that a mesh axis runs over, the one named last changes fastest.
Arguments:
- g_lesser: bfloat16 [2, 512, 2048], P(None, 'energy', 'elem'), may hold values from -6 to 6
- g_greater: bfloat16 [2, 512, 2048], P(None, 'energy', 'elem'), may hold values from -6 to 6
- send_rows: int32 [4, 8, 4, 32], P('elem'), may hold values from 0 to 63, as said below
- partner_slot: int32 [2048], P('elem'), may hold values from 0 to 127, as said below
Outputs:
- polarization_lesser: bfloat16 [2, 512, 2048], P(None, 'energy', 'elem')
- polarization_greater: bfloat16 [2, 512, 2048], P(None, 'energy', 'elem')
Inputs may be any that keep to these rules, and one draw needn't show every extreme that they name: partner is an involution on the elements that keeps the element piece n. The groups fall into two halves of 2 groups; for a sending group b and element piece n, send_rows[b, n, a, :] lists 32 distinct rows when a lies in b's half (b itself included) and zeros otherwise; every row of that piece of the sender appears exactly once over all receivers of its half. `partner_slot`: every slot named points into a receiving group's half and to a slot that carries a row; the 64 elements of one element piece of a group name 64 distinct slots.
All inputs are finite; a program needn't handle non-finite values.
Results may differ from a plain program's by a relative error of at most 0.001.
Values may be sent and summed in bfloat16 or wider, within the bound.
No kernel may reach another device: no remote copies, remote signals or barrier semaphores. Data moves between devices by JAX's collectives and lax.ppermute only.
A program may use at most 64 MiB of HBM per device.

v0:
```python
import functools
import math

import jax
import jax.numpy as jnp
import numpy as np
from jax import lax
from jax.experimental import pallas as pl
from jax.experimental.pallas import tpu as pltpu
from jax.sharding import PartitionSpec as P

BF16 = jnp.bfloat16
F32 = jnp.float32
VMEM_BYTES = 24 * 1024 * 1024
COLLECT_FLOPS = 2**33
RARE = 15


def fourier_tables(length):
    half = length // 2
    steps = np.arange(half)[:, None] * np.arange(length)[None, :] % length
    angle = steps * (2.0 * math.pi / length)
    sines = np.sin(angle)
    sines[0] = 1.0 - 2.0 * (np.arange(length) % 2)
    table = np.concatenate([np.cos(angle), sines], 0)

    def split(values):
        high = values.astype(np.float32).astype(jnp.bfloat16)
        low = (values - high.astype(np.float64)).astype(np.float32).astype(jnp.bfloat16)
        return np.stack([high, low])

    return np.concatenate([split(table), split(table.T)])


def pack_kernel(lesser_ref, greater_ref, out_ref):
    pieces, _, _, lanes = out_ref.shape
    width = lanes // 2
    for n in range(pieces):
        cols = slice(n * width, (n + 1) * width)
        out_ref[n] = jnp.concatenate([lesser_ref[:, :, cols], greater_ref[:, :, cols]], axis=-1)


def unpack_kernel(in_ref, lesser_ref, greater_ref):
    pieces, _, _, lanes = in_ref.shape
    width = lanes // 2
    per_tile = max(1, 128 // width)
    for first in range(0, pieces, per_tile):
        group = range(first, min(first + per_tile, pieces))
        cols = slice(first * width, (group[-1] + 1) * width)
        lesser_ref[:, :, cols] = jnp.concatenate([in_ref[n][:, :, :width] for n in group], axis=-1)
        greater_ref[:, :, cols] = jnp.concatenate([in_ref[n][:, :, width:] for n in group], axis=-1)


def one_hot(index_row, depth):
    rows = lax.broadcasted_iota(jnp.int32, (depth, index_row.shape[-1]), 0)
    return jnp.where(rows == index_row, 1.0, 0.0).astype(BF16)


def dot(a, b):
    return lax.dot_general(a, b, (((1,), (0,)), ((), ())), preferred_element_type=F32)


def rows_of(ref, part):
    blocks, _, energies, lanes = ref.shape
    return ref[:, part].reshape(blocks * energies, lanes)


def forward_sums(table_ref, signals):
    return dot(table_ref[0], signals) + dot(table_ref[1], signals)


def correlate(near, far, table_ref):
    half = near.shape[0] // 2
    length = near.shape[0]
    lanes = near.shape[1] // 2

    def parts(sums):
        return [sums[i * half : (i + 1) * half, j * lanes : (j + 1) * lanes] for i in range(2) for j in range(2)]

    a_re, a_im, b_re, b_im = parts(near)
    c_re, c_im, d_re, d_im = parts(far)
    first = lax.broadcasted_iota(jnp.int32, (half, lanes), 0) == 0
    ac_re, ac_im = a_re * c_re - a_im * c_im, a_re * c_im + a_im * c_re
    bd_re, bd_im = b_re * d_re - b_im * d_im, b_re * d_im + b_im * d_re
    u_re = jnp.where(first, 0.5 * ac_re, ac_re + bd_re)
    u_im = jnp.where(first, 0.5 * ac_im, ac_im + bd_im)
    v_re = jnp.where(first, 0.5 * bd_re, b_re * c_re - b_im * c_im - (a_re * d_re - a_im * d_im))
    v_im = jnp.where(first, 0.5 * bd_im, b_re * c_im + b_im * c_re - (a_re * d_im + a_im * d_re))
    top = jnp.concatenate([u_im, -u_re], axis=-1)
    bottom = jnp.concatenate([v_im, -v_re], axis=-1)
    products = jnp.concatenate([top, bottom], axis=0)
    high = products.astype(BF16)
    low = (products - high.astype(F32)).astype(BF16)
    back = dot(table_ref[2], high) + (dot(table_ref[2], low) + dot(table_ref[3], high))
    return (back * (2.0 / (length * math.sqrt(length)))).astype(BF16)


def correlate_kernel(index_ref, own_ref, far_ref, table_ref, out_ref):
    blocks, _, energies, lanes = own_ref.shape
    far = far_ref[...]
    own, partner = [], []
    for part in range(2):
        pick_far = one_hot(index_ref[part : part + 1, :], far.shape[-1])
        own.append(rows_of(own_ref, part))
        partner.append(dot(far, pick_far).astype(BF16))
    near = forward_sums(table_ref, jnp.concatenate(own, axis=-1))
    result = correlate(near, forward_sums(table_ref, jnp.concatenate(partner, axis=-1)), table_ref)
    for part in range(2):
        out_ref[:, part] = result[:, part * lanes : (part + 1) * lanes].reshape(blocks, energies, lanes)


def call(kernel, out_shape, flops, *args, scratch=(), in_hbm=(), out_smem=()):
    many = isinstance(out_shape, (list, tuple))
    outs = list(out_shape) if many else [out_shape]
    moved = sum(math.prod(v.shape) * v.dtype.itemsize for v in [*args, *outs])


    def specs(values, elsewhere, space):
        return [pl.BlockSpec(memory_space=space if i in elsewhere else pltpu.VMEM) for i in range(len(values))]

    out_specs = specs(outs, out_smem, pltpu.SMEM)
    args = [pltpu.with_memory_space_constraint(v, pltpu.HBM) if i in in_hbm else v for i, v in enumerate(args)]
    return pl.pallas_call(
        kernel,
        out_shape=out_shape,
        in_specs=specs(args, in_hbm, pltpu.HBM),
        out_specs=out_specs if many else out_specs[0],
        scratch_shapes=list(scratch),
        compiler_params=pltpu.CompilerParams(vmem_limit_bytes=VMEM_BYTES),
        cost_estimate=pl.CostEstimate(flops=flops, bytes_accessed=moved, transcendentals=0),
    )(*args)


def place():
    me = lax.axis_index("energy")
    return me // 2, me % 2


def columns_of(chip, width):
    return pl.ds(pl.multiple_of(chip * 2 * width, 2 * width), 2 * width)


def distances(lists_ref, plan_ref):
    pieces, groups, _ = lists_ref.shape
    group = lax.axis_index("elem")
    distance = []
    for n in range(pieces):
        found = jnp.int32(0)
        for i in range(groups):
            filled = lists_ref[n, i, 0] + lists_ref[n, i, 1] > 0
            found = found + jnp.where(jnp.logical_and(filled, group != i), group ^ i, 0)
        distance.append(found)
    near = [jnp.where(d == 1, 1, 0) for d in distance]
    middle = [jnp.where(d == 2, 1, 0) for d in distance]
    count_near, count_middle = sum(near), sum(middle)
    code = count_near * (pieces + 1) + count_middle
    number = jnp.int32(0)
    for i, (near_count, middle_count) in enumerate(counts_of(pieces)):
        number = jnp.where(code == near_count * (pieces + 1) + middle_count, i, number)
    seen_near, seen_middle, seen_far = jnp.int32(0), count_near, count_near + count_middle
    for n in range(pieces):
        far = 1 - near[n] - middle[n]
        rank = near[n] * seen_near + middle[n] * seen_middle + far * seen_far
        seen_near, seen_middle, seen_far = seen_near + near[n], seen_middle + middle[n], seen_far + far
        line = jnp.where(number < RARE, pieces - 1 - rank, 2 * (rank % (pieces // 2)) + 1 - rank // (pieces // 2))
        plan_ref[line] = jnp.int32(n)
        plan_ref[pieces + n] = line
    plan_ref[2 * pieces] = number


def counts_of(pieces):
    counts = [(near, middle) for near in range(pieces + 1) for middle in range(pieces + 1 - near)]
    return sorted(counts, key=lambda c: (math.comb(pieces, c[0]) * math.comb(pieces - c[0], c[1]), c))


def over_elem(number, values, after, *args):
    pieces, groups = lax.axis_size("energy"), lax.axis_size("elem")

    def branch(number, near, middle):
        ranked = [1] * near + [2] * middle + [3] * (pieces - near - middle)
        rank = [pieces - 1 - n if number < RARE else n // 2 + pieces // 2 * (1 - n % 2) for n in range(pieces)]
        by_line = [ranked[rank[n]] for n in range(pieces)]
        pairs = [(n * groups + i, n * groups + (i ^ by_line[n])) for n in range(pieces) for i in range(groups)]
        return lambda sent, *args: after(lax.ppermute(sent, ("energy", "elem"), pairs), *args)

    return lax.switch(number, [branch(i, *counts) for i, counts in enumerate(counts_of(pieces))], values, *args)


def split_kernel(lists_ref, slots_ref, lesser_ref, greater_ref, *refs):
    (beside_ref, keep_ref, give_ref, number_ref, lines_ref, rows_ref, spots_ref) = refs[:7]
    lesser, greater, lists, slots, packed, scalars, plan_ref, sems = refs[7:]
    chip, core = place()
    pairs = [(lists_ref, scalars), (lists_ref, lists), (slots_ref, slots)]
    tile = keep_ref.shape[-1]
    for first in range(0, lesser.shape[-1], tile):
        cols = pl.ds(first, tile)
        pairs += [(source.at[:, :, cols], target.at[:, :, cols]) for source, target in ((lesser_ref, lesser), (greater_ref, greater))]
    copies = [pltpu.make_async_copy(source, target, sems.at[i]) for i, (source, target) in enumerate(pairs)]
    for copy in copies:
        copy.start()
    for copy in copies[:3]:
        copy.wait()
    distances(scalars, plan_ref)
    pieces = packed.shape[0]
    number_ref[0] = plan_ref[2 * pieces]
    lines_ref[...] = jnp.full(lines_ref.shape, sum(plan_ref[pieces + n] * 8**n for n in range(pieces)), jnp.int32)
    piece = plan_ref[2 * chip + core]
    rows_ref[...] = lists[piece]
    spots_ref[0:1, :] = slots[pl.ds(piece // 2, 1), :]
    spots_ref[1:2, :] = jnp.full((1, spots_ref.shape[1]), piece % 2, jnp.int32)
    for copy in copies[3:]:
        copy.wait()
    width = packed.shape[-1] // 2
    for n in range(pieces):
        cols = slice(n * width, (n + 1) * width)
        packed[n] = jnp.concatenate([lesser[:, :, cols], greater[:, :, cols]], axis=-1)
    for which in range(2):
        beside_ref[which] = packed[plan_ref[2 * (chip ^ 2) + which]]
    for i, j in enumerate((0, 1, 3)):
        keep_ref[i] = packed[plan_ref[2 * (chip ^ j) + core]]
        give_ref[i] = packed[plan_ref[2 * (chip ^ j) + 1 - core]]


def swap(values, axis, bit):
    return lax.ppermute(values, axis, [(i, i ^ bit) for i in range(lax.axis_size(axis))])


def collect_kernel(keep_ref, got_ref, diagonal_ref, across_ref, out_ref):
    out_ref[0], out_ref[1] = keep_ref[0], got_ref[0]
    for which in range(2):
        out_ref[2 + which] = across_ref[which]
        out_ref[4 + which] = diagonal_ref[which]


def over_energy(first, keep, give):
    beside = swap(first, "energy", 4)
    got = swap(give, "energy", 1)
    diagonal = swap(jnp.stack([keep[2], got[2]]), "energy", 6)
    across = swap(jnp.stack([keep[1], got[1]]), "energy", 2)
    early = jax.ShapeDtypeStruct((6, *keep.shape[1:]), BF16)
    early = call(collect_kernel, early, COLLECT_FLOPS, keep, got, diagonal, across)
    return early, beside, swap(beside, "energy", 1)


def blocks_of(refs, core):
    early_ref, beside_ref, beside_other_ref = refs
    early = [(lambda i=i: early_ref[i], lambda i=i: early_ref[i + 1]) for i in (0, 2, 4)]
    return [early[0], early[1], (lambda: beside_ref[core], lambda: beside_other_ref[core]), early[2]]


def lane_row(lanes):
    return lax.broadcasted_iota(jnp.int32, (1, lanes), 1)


def energies_of(device, energies):
    return pl.ds(pl.multiple_of(device * energies, energies), energies)


def repeat(values, index_row):
    return dot(values.astype(F32).astype(BF16), one_hot(index_row, values.shape[-1])).astype(jnp.int32)


def index_kernel(rows_ref, spots_ref, picks_ref):
    group = lax.axis_index("elem")
    lanes = picks_ref.shape[-1]
    width, cap = lanes // 2, lanes // 4
    lane = lane_row(lanes)
    lists = repeat(rows_ref[...], lane % cap)
    ids = lax.broadcasted_iota(jnp.int32, lists.shape, 0)
    greater = jnp.where(lane // cap % 2 == 1, width, 0)
    near_rows = jnp.sum(jnp.where(ids == group, lists, 0), axis=0, keepdims=True) + greater
    far_rows = jnp.sum(jnp.where(ids == group, 0, lists), axis=0, keepdims=True) + greater
    slots = spots_ref[0:1, :]
    twice = [repeat(slots, half * width + lane % width) for half in range(2)]
    slots = jnp.where(spots_ref[1:2, :] == 0, *twice)
    source = slots // cap
    spot = slots - source * cap + jnp.where(lane < width, cap, 0)
    near = one_hot(jnp.where(lane < 2 * cap, near_rows, -1), lanes)
    picks_ref[0] = dot(near, one_hot(jnp.where(source == group, spot, -1), lanes)).astype(BF16)
    for part in range(2):
        picks_ref[1 + part] = one_hot(jnp.where(source == group, -1, spot + 2 * cap * part), lanes)
        picks_ref[3 + part] = one_hot(jnp.where(lane // (2 * cap) == part, far_rows, -1), lanes)


def gather_kernel(picks_ref, *refs):
    in_refs, (signals_ref, sent_ref) = refs[:3], refs[3:]
    chip, core = place()
    energies, lanes = in_refs[0].shape[2:]
    for j, pair in enumerate(blocks_of(in_refs, core)):
        for which, block in enumerate(pair):
            values = block()
            rows = energies_of(2 * (chip ^ j) + (core if which == 0 else 1 - core), energies)
            for part in range(2):
                signals_ref[rows, part * lanes : (part + 1) * lanes] = values[part]
    sent_ref[...] = (dot(signals_ref[:, :lanes], picks_ref[3]) + dot(signals_ref[:, lanes:], picks_ref[4])).astype(BF16)


def own_kernel(signals_ref, picks_ref, table_ref, sums_ref, partner_ref, held_ref, sems):
    lanes = picks_ref.shape[-1]
    steps = sems.shape[0] // 4
    height = table_ref.shape[1] // steps
    copies = []
    for i in range(4 * steps):
        rows = pl.ds(i % steps * height, height)
        copies.append(pltpu.make_async_copy(table_ref.at[i // steps, rows], held_ref.at[i // steps, rows], sems.at[i]))
    for copy in copies:
        copy.start()
    for part in range(2):
        cols = slice(part * lanes, (part + 1) * lanes)
        partner_ref[:, cols] = dot(signals_ref[:, cols], picks_ref[0]).astype(BF16)
    for copy in copies:
        copy.wait()
    sums_ref[...] = forward_sums(held_ref, signals_ref[...])


def pick_kernel(near_ref, far_ref, picks_ref, partner_ref):
    lanes = picks_ref.shape[-1]
    far = far_ref[...]
    for part in range(2):
        cols = slice(part * lanes, (part + 1) * lanes)
        partner_ref[:, cols] = (near_ref[:, cols].astype(F32) + dot(far, picks_ref[1 + part])).astype(BF16)


def exchange_kernel(sums_ref, partner_ref, table_ref, *refs):
    (beside_ref, keep_ref, give_ref), (held,) = refs[:3], refs[3:]
    chip, core = place()
    energies, lanes = keep_ref.shape[2:]
    held[...] = correlate(sums_ref[...], forward_sums(table_ref, partner_ref[...]), table_ref)

    def block(j, core):
        rows = energies_of(2 * (chip ^ j) + core, energies)
        return [held[rows, part * lanes : (part + 1) * lanes] for part in range(2)]

    for which in range(2):
        beside_ref[which, 0], beside_ref[which, 1] = block(2, which)
    for i, j in enumerate((0, 1, 3)):
        keep_ref[i, 0], keep_ref[i, 1] = block(j, core)
        give_ref[i, 0], give_ref[i, 1] = block(j, 1 - core)


def join_kernel(lines_ref, *refs):
    in_refs, (lesser_ref, greater_ref, held) = refs[:3], refs[3:]
    chip, core = place()
    width = held.shape[-1] // 2
    for j, (mine, other) in enumerate(blocks_of(in_refs, core)):
        held[2 * (chip ^ j) + core] = mine()
        held[2 * (chip ^ j) + 1 - core] = other()
    lines = jnp.max(lines_ref[...])
    for n in range(0, held.shape[0], 2):
        even, odd = held[lines // 8**n % 8], held[lines // 8 ** (n + 1) % 8]
        cols = slice(n * width, (n + 2) * width)
        lesser_ref[:, :, cols] = jnp.concatenate([even[..., :width], odd[..., :width]], axis=-1)
        greater_ref[:, :, cols] = jnp.concatenate([even[..., width:], odd[..., width:]], axis=-1)


def four_chips(g_lesser, g_greater, send_rows, partner_slot):
    _, energies, group_rows = g_lesser.shape
    cap = send_rows.shape[-1]
    lanes = 4 * cap
    length = 8 * energies
    pair = jax.ShapeDtypeStruct((2, 2, energies, lanes), BF16)
    three = jax.ShapeDtypeStruct((3, 2, energies, lanes), BF16)
    leaving = [pair, three, three]
    column = jax.ShapeDtypeStruct((length, lanes), BF16)
    whole = jax.ShapeDtypeStruct((length, 2 * lanes), BF16)
    slots = partner_slot.reshape(4, lanes)
    table = jnp.asarray(fourier_tables(length))

    scratch = [
        pltpu.VMEM(g_lesser.shape, BF16),
        pltpu.VMEM(g_lesser.shape, BF16),
        pltpu.VMEM(send_rows.shape[1:], jnp.int32),
        pltpu.VMEM(slots.shape, jnp.int32),
        pltpu.VMEM((8, 2, energies, lanes), BF16),
        pltpu.SMEM(send_rows.shape[1:], jnp.int32),
        pltpu.SMEM((17,), jnp.int32),
        pltpu.SemaphoreType.DMA((11,)),
    ]
    more = [
        jax.ShapeDtypeStruct((1,), jnp.int32),
        jax.ShapeDtypeStruct((8, lanes), jnp.int32),
        jax.ShapeDtypeStruct((4, cap), jnp.int32),
        jax.ShapeDtypeStruct((2, lanes), jnp.int32),
    ]
    beside, keep, give, number, lines, rows, spots = call(
        split_kernel,
        leaving + more,
        2**24,
        send_rows[0],
        slots,
        g_lesser,
        g_greater,
        scratch=scratch,
        in_hbm=(0, 1, 2, 3),
        out_smem=(3,),
    )
    picks = call(index_kernel, jax.ShapeDtypeStruct((5, lanes, lanes), BF16), 2**24, rows, spots)
    beside, picks = lax.optimization_barrier((beside, picks))

    signals, sent = call(gather_kernel, [whole, column], 2**26, picks, *over_energy(beside, keep, give))

    def after(far, signals, picks, table):
        shapes = [jax.ShapeDtypeStruct(whole.shape, F32), whole, jax.ShapeDtypeStruct(table.shape, BF16)]
        sems = [pltpu.SemaphoreType.DMA((16,))]
        sums, near, held = call(own_kernel, shapes, 2**29, signals, picks, table, scratch=sems, in_hbm=(2,))
        return sums, call(pick_kernel, whole, 2**26, near, far, picks), held

    sums, partner, held = over_elem(number[0], sent, after, signals, picks, table)
    results = call(exchange_kernel, leaving, 2**30, sums, partner, held, scratch=[pltpu.VMEM(whole.shape, BF16)])
    out = jax.ShapeDtypeStruct((2, energies, group_rows), BF16)
    scratch = [pltpu.VMEM((8, 2, energies, lanes), BF16)]
    return tuple(call(join_kernel, [out, out], 0, lines, *over_energy(*results), scratch=scratch))


def any_mesh(g_lesser, g_greater, send_rows, partner_slot):
    piece = lax.axis_index("energy")
    pieces = lax.axis_size("energy")
    _, energies, group_rows = g_lesser.shape
    groups, cap = send_rows.shape[2:]
    width = group_rows // pieces
    lanes = 2 * width
    length = pieces * energies
    packed_shape = jax.ShapeDtypeStruct((pieces, 2, energies, lanes), BF16)
    packed = call(pack_kernel, packed_shape, 0, g_lesser, g_greater)
    own = lax.all_to_all(packed, "energy", split_axis=0, concat_axis=0, tiled=True)
    rows = lax.dynamic_index_in_dim(send_rows[0], piece, 0, keepdims=False).reshape(-1)
    slots = lax.dynamic_slice_in_dim(partner_slot, piece * width, width, 0)
    pick = (jnp.arange(width, dtype=jnp.int32)[:, None] == rows[None, :]).astype(BF16)
    split = own.reshape(pieces, 2, energies, 2, width)
    outgoing = jnp.einsum("pceds,sm->mpced", split, pick, preferred_element_type=F32).astype(BF16)
    incoming = lax.all_to_all(outgoing, "elem", split_axis=0, concat_axis=0, tiled=True)
    table_width = groups * cap
    far = jnp.transpose(incoming, (1, 3, 2, 4, 0)).reshape(length, 4 * table_width)
    index = jnp.concatenate([slots + table_width, slots])
    index = jnp.stack([index, index + 2 * table_width])
    result = call(
        correlate_kernel,
        packed_shape,
        2 * length * length * lanes * 14,
        index,
        own,
        far,
        jnp.asarray(fourier_tables(length)),
    )
    back = lax.all_to_all(result, "energy", split_axis=0, concat_axis=0, tiled=True)
    out = jax.ShapeDtypeStruct((2, energies, group_rows), BF16)
    return tuple(call(unpack_kernel, [out, out], 0, back))


def shards(g_lesser, g_greater, send_rows, partner_slot):
    _, pieces, groups, cap = send_rows.shape
    fits = pieces == 8 and groups == 4 and cap == 32 and partner_slot.shape[0] == 512
    path = four_chips if fits else any_mesh
    return path(g_lesser, g_greater, send_rows, partner_slot)


def solution(mesh):
    in_specs = (
        P(None, "energy", "elem"),
        P(None, "energy", "elem"),
        P("elem", None, None, None),
        P("elem"),
    )
    out_specs = (P(None, "energy", "elem"), P(None, "energy", "elem"))
    return jax.shard_map(shards, mesh=mesh, in_specs=in_specs, out_specs=out_specs, check_vma=False)
```

profile of v0, /device:TPU:0, one launch (start us, length us, event | category | flops | bytes accessed | tf_op | source)
XLA Modules:
  0.0 30.2 jit_solution(9319047162063730094)
XLA Ops:
  0.6 1.8 %shard_map.68 = (bf16[2,2,64,128]{3,2,1,0:T(8,128)(2,1)S(1)}, bf16[3,2,64,128]{3,2,1,0:T(8,128)(2,1)S(1)}, bf16[3,2,64,128]{3,2,1,0:T(8,128)(2,1)S(1)}, s32[1]{0...) custom-call(s32[8,4,32]{2,1,0:T(4,128)} %bitcast.3, s32[4,128]{1,0:T(4,128)} %bitcast.4, ...), custom_call_target="tpu_custom_call" | custom-call | flops 16777216 | bytes 536068 | tf_op jit(solution)/shard_map/pallas_call | solution.py:123
  2.4 0.5 %collective-permute-start.45 = (bf16[3,2,64,128]{3,2,1,0:T(8,128)(2,1)S(1)}, bf16[3,2,64,128]{3,2,1,0:T(8,128)(2,1)S(1)}, u32[]{:S(2)}, u32[]{:S(2)}) collective-permute-start(bf16[3,2,64,128]{3,2,1,0:T(8,128)(2,1)S(1)} %get-tuple-element.701), channel_id=1, source_target_pairs={{0,4},{4,0},{8,12},{12,8},{16,20},{20,16},{24,28},{28,24},{1,5},{5... | collective-permute-start | bytes 294920 | tf_op jit(solution)/shard_map/ppermute | solution.py:225
  2.9 0.3 %shard_map.69.picks_ref = bf16[5,128,128]{2,1,0:T(8,128)(2,1)S(1)} custom-call(s32[4,32]{1,0:T(4,128)S(1)} %get-tuple-element.697.rows_ref, s32[2,128]{1,0:T(2,128)S(1)} %get-tuple-element.698.spots_ref), custom_call_target="tpu_custom_call" | custom-call | flops 16777216 | bytes 165376 | tf_op jit(solution)/shard_map/pallas_call | solution.py:123
  3.2 2.6 %collective-permute-start.48 = (bf16[2,2,64,128]{3,2,1,0:T(8,128)(2,1)S(1)}, bf16[2,2,64,128]{3,2,1,0:T(8,128)(2,1)S(1)}, u32[]{:S(2)}, u32[]{:S(2)}) collective-permute-start(bf16[2,2,64,128]{3,2,1,0:T(8,128)(2,1)S(1)} %get-tuple-element.702), channel_id=1, source_target_pairs={{0,16},{4,20},{8,24},{12,28},{16,0},{20,4},{24,8},{28,12},{1,17},{... | collective-permute-start | bytes 196616 | tf_op jit(solution)/shard_map/ppermute | solution.py:225
  5.9 1.9 %collective-permute-start.46 = (bf16[2,2,64,128]{3,2,1,0:T(8,128)(2,1)S(1)}, bf16[2,2,64,128]{3,2,1,0:T(8,128)(2,1)S(1)}, u32[]{:S(2)}, u32[]{:S(2)}) collective-permute-start(bf16[2,2,64,128]{3,2,1,0:T(8,128)(2,1)S(1)} %pad_maximum_fusion), channel_id=1, source_target_pairs={{0,24},{4,28},{8,16},{12,20},{16,8},{20,12},{24,0},{28,4},{1,25},{... | collective-permute-start | bytes 196616 | tf_op jit(solution)/shard_map/ppermute | solution.py:225
  7.8 0.6 %collective-permute-start.47 = (bf16[2,2,64,128]{3,2,1,0:T(8,128)(2,1)S(1)}, bf16[2,2,64,128]{3,2,1,0:T(8,128)(2,1)S(1)}, u32[]{:S(2)}, u32[]{:S(2)}) collective-permute-start(bf16[2,2,64,128]{3,2,1,0:T(8,128)(2,1)S(1)} %pad_maximum_fusion.1), channel_id=1, source_target_pairs={{0,8},{4,12},{8,0},{12,4},{16,24},{20,28},{24,16},{28,20},{1,9},{5... | collective-permute-start | bytes 196616 | tf_op jit(solution)/shard_map/ppermute | solution.py:225
  9.0 0.1 collective-permute-start.49
  9.1 2.3 %collective-permute-done.46.diagonal_ref = bf16[2,2,64,128]{3,2,1,0:T(8,128)(2,1)S(1)} collective-permute-done((bf16[2,2,64,128]{3,2,1,0:T(8,128)(2,1)S(1)}, bf16[2,2,64,128]{3,2,1,0:T(8,128)(2,1)S(1)}, u32[]{:S(2)}, u32[]{:S(2)}) %collective-permute-start.46) | collective-permute-done | bytes 65568 | tf_op jit(solution)/shard_map/ppermute | solution.py:225
  11.4 0.7 %collective-permute-done.47.across_ref = bf16[2,2,64,128]{3,2,1,0:T(8,128)(2,1)S(1)} collective-permute-done((bf16[2,2,64,128]{3,2,1,0:T(8,128)(2,1)S(1)}, bf16[2,2,64,128]{3,2,1,0:T(8,128)(2,1)S(1)}, u32[]{:S(2)}, u32[]{:S(2)}) %collective-permute-start.47) | collective-permute-done | bytes 65568 | tf_op jit(solution)/shard_map/ppermute | solution.py:225
  12.1 0.2 shard_map.71
  12.4 7.4 %conditional.1 = (f32[512,256]{1,0:T(8,128)S(1)}, bf16[512,256]{1,0:T(8,128)(2,1)S(1)}, bf16[4,512,512]{2,1,0:T(8,128)(2,1)S(1)}) conditional(s32[]{:T(128)} %bitcast.2, (bf16[512,256]{1,0:T(8,128)(2,1)S(1)}, bf16[5,128,128]{2,1,0:T(8,128)(2,1)S(1)}, bf16[4,512,512]{2,1,0:T(8,128)(2,1)}, ...), branch_computations={%region_0.0_spmd, %region_1.0_spmd, %region_2.0_spmd, %region_3.0_... | conditional | flops 603979776 | bytes 6750272 | solution.py:186
  12.6 3.7 %collective-permute-start.35 = (bf16[512,128]{1,0:T(8,128)(2,1)S(1)}, bf16[512,128]{1,0:T(8,128)(2,1)S(1)}, u32[]{:S(2)}, u32[]{:S(2)}) collective-permute-start(bf16[512,128]{1,0:T(8,128)(2,1)S(1)} %get-tuple-element.610), channel_id=1, source_target_pairs={{0,3},{1,2},{2,1},{3,0},{4,5},{5,4},{6,7},{7,6},{8,11},{9,10},{10,... | collective-permute-start | bytes 393224 | tf_op jit(solution)/shard_map/cond/branch_35_fun/ppermute | solution.py:184
  16.3 2.2 %branch_35_fun.2 = (f32[512,256]{1,0:T(8,128)S(1)}, bf16[512,256]{1,0:T(8,128)(2,1)S(1)}, bf16[4,512,512]{2,1,0:T(8,128)(2,1)S(1)}) custom-call(bf16[512,256]{1,0:T(8,128)(2,1)S(1)} %get-tuple-element.605.signals_ref, bf16[5,128,128]{2,1,0:T(8,128)(2,1)S(1)} %get-tuple-element.606.picks_ref, bf16[4,512,512]{2,1,0:T(8,128)(2,1)} %get-tuple-element.607.table_ref), custom_call_target="tpu_custom_call" | custom-call | flops 536870912 | bytes 5406720 | tf_op jit(solution)/shard_map/cond/branch_35_fun/pallas_call | solution.py:123
  18.5 1.1 %collective-permute-done.35.far_ref = bf16[512,128]{1,0:T(8,128)(2,1)S(1)} collective-permute-done((bf16[512,128]{1,0:T(8,128)(2,1)S(1)}, bf16[512,128]{1,0:T(8,128)(2,1)S(1)}, u32[]{:S(2)}, u32[]{:S(2)}) %collective-permute-start.35) | collective-permute-done | bytes 131104 | tf_op jit(solution)/shard_map/cond/branch_35_fun/ppermute | solution.py:184
  19.6 0.2 branch_35_fun.3
  19.8 1.6 %shard_map.72 = (bf16[2,2,64,128]{3,2,1,0:T(8,128)(2,1)S(1)}, bf16[3,2,64,128]{3,2,1,0:T(8,128)(2,1)S(1)}, bf16[3,2,64,128]{3,2,1,0:T(8,128)(2,1)S(1)}) custom-call(f32[512,256]{1,0:T(8,128)S(1)} %get-tuple-element.705.sums_ref, bf16[512,256]{1,0:T(8,128)(2,1)S(1)} %get-tuple-element.706.partner_ref, bf16[4,512,512]{2,1,0:T(8,128)(2,1)S(1)} %get-tuple-element.707.table_ref), custom_call_target="tpu_custom_call" | custom-call | flops 1073741824 | bytes 3145728 | tf_op jit(solution)/shard_map/pallas_call | solution.py:123
  21.4 0.1 collective-permute-start.50
  21.5 1.2 %collective-permute-start.53 = (bf16[2,2,64,128]{3,2,1,0:T(8,128)(2,1)S(1)}, bf16[2,2,64,128]{3,2,1,0:T(8,128)(2,1)S(1)}, u32[]{:S(2)}, u32[]{:S(2)}) collective-permute-start(bf16[2,2,64,128]{3,2,1,0:T(8,128)(2,1)S(1)} %get-tuple-element.710), channel_id=1, source_target_pairs={{0,16},{4,20},{8,24},{12,28},{16,0},{20,4},{24,8},{28,12},{1,17},{... | collective-permute-start | bytes 196616 | tf_op jit(solution)/shard_map/ppermute | solution.py:225
  22.8 1.9 %collective-permute-start.51 = (bf16[2,2,64,128]{3,2,1,0:T(8,128)(2,1)S(1)}, bf16[2,2,64,128]{3,2,1,0:T(8,128)(2,1)S(1)}, u32[]{:S(2)}, u32[]{:S(2)}) collective-permute-start(bf16[2,2,64,128]{3,2,1,0:T(8,128)(2,1)S(1)} %pad_maximum_fusion.2), channel_id=1, source_target_pairs={{0,24},{4,28},{8,16},{12,20},{16,8},{20,12},{24,0},{28,4},{1,25},{... | collective-permute-start | bytes 196616 | tf_op jit(solution)/shard_map/ppermute | solution.py:225
  24.7 0.9 %collective-permute-start.52 = (bf16[2,2,64,128]{3,2,1,0:T(8,128)(2,1)S(1)}, bf16[2,2,64,128]{3,2,1,0:T(8,128)(2,1)S(1)}, u32[]{:S(2)}, u32[]{:S(2)}) collective-permute-start(bf16[2,2,64,128]{3,2,1,0:T(8,128)(2,1)S(1)} %pad_maximum_fusion.3), channel_id=1, source_target_pairs={{0,8},{4,12},{8,0},{12,4},{16,24},{20,28},{24,16},{28,20},{1,9},{5... | collective-permute-start | bytes 196616 | tf_op jit(solution)/shard_map/ppermute | solution.py:225
  25.5 0.5 %collective-permute-done.53.refs_1_ = bf16[2,2,64,128]{3,2,1,0:T(8,128)(2,1)S(1)} collective-permute-done((bf16[2,2,64,128]{3,2,1,0:T(8,128)(2,1)S(1)}, bf16[2,2,64,128]{3,2,1,0:T(8,128)(2,1)S(1)}, u32[]{:S(2)}, u32[]{:S(2)}) %collective-permute-start.53) | collective-permute-done | bytes 65568 | tf_op jit(solution)/shard_map/ppermute | solution.py:225
  26.0 2.5 %collective-permute-done.51.diagonal_ref = bf16[2,2,64,128]{3,2,1,0:T(8,128)(2,1)S(1)} collective-permute-done((bf16[2,2,64,128]{3,2,1,0:T(8,128)(2,1)S(1)}, bf16[2,2,64,128]{3,2,1,0:T(8,128)(2,1)S(1)}, u32[]{:S(2)}, u32[]{:S(2)}) %collective-permute-start.51) | collective-permute-done | bytes 65568 | tf_op jit(solution)/shard_map/ppermute | solution.py:225
  28.5 0.6 %collective-permute-done.52.across_ref = bf16[2,2,64,128]{3,2,1,0:T(8,128)(2,1)S(1)} collective-permute-done((bf16[2,2,64,128]{3,2,1,0:T(8,128)(2,1)S(1)}, bf16[2,2,64,128]{3,2,1,0:T(8,128)(2,1)S(1)}, u32[]{:S(2)}, u32[]{:S(2)}) %collective-permute-start.52) | collective-permute-done | bytes 65568 | tf_op jit(solution)/shard_map/ppermute | solution.py:225
  29.1 1.0 %shard_map.74 = (bf16[2,64,512]{2,1,0:T(8,128)(2,1)}, bf16[2,64,512]{2,1,0:T(8,128)(2,1)}) custom-call(s32[8,128]{1,0:T(8,128)S(1)} %get-tuple-element.694.lines_ref, bf16[6,2,64,128]{3,2,1,0:T(8,128)(2,1)S(1)} %shard_map.73.refs_0_, bf16[2,2,64,128]{3,2,1,0:T(8,128)(2,1)S(1)} %collective-permute-done.53.refs_1_, ...), custom_call_target="tpu_custom_call" | custom-call | bytes 593920 | tf_op jit(solution)/shard_map/pallas_call | solution.py:123
  (16 shorter events, 0.2 us)
Async XLA Ops:
  2.4 3.4 %collective-permute-start.45 = (bf16[3,2,64,128]{3,2,1,0:T(8,128)(2,1)S(1)}, bf16[3,2,64,128]{3,2,1,0:T(8,128)(2,1)S(1)}, u32[]{:S(2)}, u32[]{:S(2)}) collective-permute-start(bf16[3,2,64,128]{3,2,1,0:T(8,128)(2,1)S(1)} %get-tuple-element.701), channel_id=1, source_target_pairs={{0,4},{4,0},{8,12},{12,8},{16,20},{20,16},{24,28},{28,24},{1,5},{5... | collective-permute-start | bytes 294920 | tf_op jit(solution)/shard_map/ppermute | solution.py:225
  3.2 5.8 %collective-permute-start.48 = (bf16[2,2,64,128]{3,2,1,0:T(8,128)(2,1)S(1)}, bf16[2,2,64,128]{3,2,1,0:T(8,128)(2,1)S(1)}, u32[]{:S(2)}, u32[]{:S(2)}) collective-permute-start(bf16[2,2,64,128]{3,2,1,0:T(8,128)(2,1)S(1)} %get-tuple-element.702), channel_id=1, source_target_pairs={{0,16},{4,20},{8,24},{12,28},{16,0},{20,4},{24,8},{28,12},{1,17},{... | collective-permute-start | bytes 196616 | tf_op jit(solution)/shard_map/ppermute | solution.py:225
  5.9 5.5 %collective-permute-start.46 = (bf16[2,2,64,128]{3,2,1,0:T(8,128)(2,1)S(1)}, bf16[2,2,64,128]{3,2,1,0:T(8,128)(2,1)S(1)}, u32[]{:S(2)}, u32[]{:S(2)}) collective-permute-start(bf16[2,2,64,128]{3,2,1,0:T(8,128)(2,1)S(1)} %pad_maximum_fusion), channel_id=1, source_target_pairs={{0,24},{4,28},{8,16},{12,20},{16,8},{20,12},{24,0},{28,4},{1,25},{... | collective-permute-start | bytes 196616 | tf_op jit(solution)/shard_map/ppermute | solution.py:225
  7.8 4.3 %collective-permute-start.47 = (bf16[2,2,64,128]{3,2,1,0:T(8,128)(2,1)S(1)}, bf16[2,2,64,128]{3,2,1,0:T(8,128)(2,1)S(1)}, u32[]{:S(2)}, u32[]{:S(2)}) collective-permute-start(bf16[2,2,64,128]{3,2,1,0:T(8,128)(2,1)S(1)} %pad_maximum_fusion.1), channel_id=1, source_target_pairs={{0,8},{4,12},{8,0},{12,4},{16,24},{20,28},{24,16},{28,20},{1,9},{5... | collective-permute-start | bytes 196616 | tf_op jit(solution)/shard_map/ppermute | solution.py:225
  9.0 3.1 %collective-permute-start.49 = (bf16[2,2,64,128]{3,2,1,0:T(8,128)(2,1)S(1)}, bf16[2,2,64,128]{3,2,1,0:T(8,128)(2,1)S(1)}, u32[]{:S(2)}, u32[]{:S(2)}) collective-permute-start(bf16[2,2,64,128]{3,2,1,0:T(8,128)(2,1)S(1)} %collective-permute-done.48.refs_1_), channel_id=1, source_target_pairs={{0,4},{4,0},{8,12},{12,8},{16,20},{20,16},{24,28},{28,24},{1,5},{5... | collective-permute-start | bytes 196616 | tf_op jit(solution)/shard_map/ppermute | solution.py:225
  12.6 6.9 %collective-permute-start.35 = (bf16[512,128]{1,0:T(8,128)(2,1)S(1)}, bf16[512,128]{1,0:T(8,128)(2,1)S(1)}, u32[]{:S(2)}, u32[]{:S(2)}) collective-permute-start(bf16[512,128]{1,0:T(8,128)(2,1)S(1)} %get-tuple-element.610), channel_id=1, source_target_pairs={{0,3},{1,2},{2,1},{3,0},{4,5},{5,4},{6,7},{7,6},{8,11},{9,10},{10,... | collective-permute-start | bytes 393224 | tf_op jit(solution)/shard_map/cond/branch_35_fun/ppermute | solution.py:184
  21.4 1.4 %collective-permute-start.50 = (bf16[3,2,64,128]{3,2,1,0:T(8,128)(2,1)S(1)}, bf16[3,2,64,128]{3,2,1,0:T(8,128)(2,1)S(1)}, u32[]{:S(2)}, u32[]{:S(2)}) collective-permute-start(bf16[3,2,64,128]{3,2,1,0:T(8,128)(2,1)S(1)} %get-tuple-element.709), channel_id=1, source_target_pairs={{0,4},{4,0},{8,12},{12,8},{16,20},{20,16},{24,28},{28,24},{1,5},{5... | collective-permute-start | bytes 294920 | tf_op jit(solution)/shard_map/ppermute | solution.py:225
  21.5 4.5 %collective-permute-start.53 = (bf16[2,2,64,128]{3,2,1,0:T(8,128)(2,1)S(1)}, bf16[2,2,64,128]{3,2,1,0:T(8,128)(2,1)S(1)}, u32[]{:S(2)}, u32[]{:S(2)}) collective-permute-start(bf16[2,2,64,128]{3,2,1,0:T(8,128)(2,1)S(1)} %get-tuple-element.710), channel_id=1, source_target_pairs={{0,16},{4,20},{8,24},{12,28},{16,0},{20,4},{24,8},{28,12},{1,17},{... | collective-permute-start | bytes 196616 | tf_op jit(solution)/shard_map/ppermute | solution.py:225
  22.8 5.7 %collective-permute-start.51 = (bf16[2,2,64,128]{3,2,1,0:T(8,128)(2,1)S(1)}, bf16[2,2,64,128]{3,2,1,0:T(8,128)(2,1)S(1)}, u32[]{:S(2)}, u32[]{:S(2)}) collective-permute-start(bf16[2,2,64,128]{3,2,1,0:T(8,128)(2,1)S(1)} %pad_maximum_fusion.2), channel_id=1, source_target_pairs={{0,24},{4,28},{8,16},{12,20},{16,8},{20,12},{24,0},{28,4},{1,25},{... | collective-permute-start | bytes 196616 | tf_op jit(solution)/shard_map/ppermute | solution.py:225
  24.7 4.4 %collective-permute-start.52 = (bf16[2,2,64,128]{3,2,1,0:T(8,128)(2,1)S(1)}, bf16[2,2,64,128]{3,2,1,0:T(8,128)(2,1)S(1)}, u32[]{:S(2)}, u32[]{:S(2)}) collective-permute-start(bf16[2,2,64,128]{3,2,1,0:T(8,128)(2,1)S(1)} %pad_maximum_fusion.3), channel_id=1, source_target_pairs={{0,8},{4,12},{8,0},{12,4},{16,24},{20,28},{24,16},{28,20},{1,9},{5... | collective-permute-start | bytes 196616 | tf_op jit(solution)/shard_map/ppermute | solution.py:225
  26.0 3.1 %collective-permute-start.54 = (bf16[2,2,64,128]{3,2,1,0:T(8,128)(2,1)S(1)}, bf16[2,2,64,128]{3,2,1,0:T(8,128)(2,1)S(1)}, u32[]{:S(2)}, u32[]{:S(2)}) collective-permute-start(bf16[2,2,64,128]{3,2,1,0:T(8,128)(2,1)S(1)} %collective-permute-done.53.refs_1_), channel_id=1, source_target_pairs={{0,4},{4,0},{8,12},{12,8},{16,20},{20,16},{24,28},{28,24},{1,5},{5... | collective-permute-start | bytes 196616 | tf_op jit(solution)/shard_map/ppermute | solution.py:225
where the time goes:
time: 30.5 us; the launch traced here: 30.2 us
  starting transfers between devices  13.3 us (44%)
  waiting for transfers between devices  7.72 us (25%)
  Pallas kernels  7.37 us (24%)
  between operations  1.41 us (5%)
    ppermute x10, starting transfers between devices, swap(): lax.ppermute(values, axis, [(i, i ^ bit) for i in range(lax.axis_size(axi...  9.67 us
    pallas_call x9, Pallas kernels, call(): pl.pallas_call(kernel, out_shape=out_shape, in_specs=specs(args, in_hbm,...  7.37 us
    ppermute x10, waiting for transfers between devices, swap(): lax.ppermute(values, axis, [(i, i ^ bit) for i in range(lax.axis_size(axi...  6.63 us
    ppermute x1, starting transfers between devices, branch(): lax.ppermute(sent, ('energy', 'elem'), pairs)  3.66 us
    ppermute x1, waiting for transfers between devices, branch(): lax.ppermute(sent, ('energy', 'elem'), pairs)  1.09 us
  transfers between devices with their start and end apart: 11, of which 7 were waited for; matrix products, arithmetic and copies ran while one was open for 0% of the time, Pallas kernels for 8%

commit v1 on v0

--- a/solution.py
+++ b/solution.py
@@ -157,12 +157,13 @@
     number = jnp.int32(0)
     for i, (near_count, middle_count) in enumerate(counts_of(pieces)):
         number = jnp.where(code == near_count * (pieces + 1) + middle_count, i, number)
+    front = jnp.where(count_near > 1, 1, 0)
     seen_near, seen_middle, seen_far = jnp.int32(0), count_near, count_near + count_middle
     for n in range(pieces):
         far = 1 - near[n] - middle[n]
         rank = near[n] * seen_near + middle[n] * seen_middle + far * seen_far
         seen_near, seen_middle, seen_far = seen_near + near[n], seen_middle + middle[n], seen_far + far
-        line = jnp.where(number < RARE, pieces - 1 - rank, 2 * (rank % (pieces // 2)) + 1 - rank // (pieces // 2))
+        line = jnp.where(number < RARE, pieces - 1 - rank, 2 * (rank % (pieces // 2)) + (rank // (pieces // 2) ^ front))
         plan_ref[line] = jnp.int32(n)
         plan_ref[pieces + n] = line
     plan_ref[2 * pieces] = number
@@ -178,7 +179,7 @@
 
     def branch(number, near, middle):
         ranked = [1] * near + [2] * middle + [3] * (pieces - near - middle)
-        rank = [pieces - 1 - n if number < RARE else n // 2 + pieces // 2 * (1 - n % 2) for n in range(pieces)]
+        rank = [pieces - 1 - n if number < RARE else n // 2 + pieces // 2 * (n % 2 ^ int(near > 1)) for n in range(pieces)]
         by_line = [ranked[rank[n]] for n in range(pieces)]
         pairs = [(n * groups + i, n * groups + (i ^ by_line[n])) for n in range(pieces) for i in range(groups)]
         return lambda sent, *args: after(lax.ppermute(sent, ("energy", "elem"), pairs), *args)

time: 30.5 us -> 30.6 us (level)
  waiting for transfers between devices: 7.72 us -> 9.51 us
  starting transfers between devices: 13.3 us -> 11.6 us
    ppermute x1, waiting for transfers between devices: 1.09 us -> 2.49 us  [branch(): lax.ppermute(sent, ('energy', 'elem'), pairs)]
    ppermute x1, starting transfers between devices: 3.66 us -> 2.65 us  [branch(): lax.ppermute(sent, ('energy', 'elem'), pairs)]
    ppermute x10, starting transfers between devices: 9.67 us -> 8.96 us  [swap(): lax.ppermute(values, axis, [(i, i ^ bit) for i in range(lax.axis_size(axi...]
    ppermute x10, waiting for transfers between devices: 6.63 us -> 7.02 us  [swap(): lax.ppermute(values, axis, [(i, i ^ bit) for i in range(lax.axis_size(axi...]
where the time goes in v1:
time: 30.6 us; the launch traced here: 30.2 us
  starting transfers between devices  11.6 us (38%)
  waiting for transfers between devices  9.51 us (31%)
  Pallas kernels  7.37 us (24%)
  between operations  1.41 us (5%)
    ppermute x10, starting transfers between devices, swap(): lax.ppermute(values, axis, [(i, i ^ bit) for i in range(lax.axis_size(axi...  8.96 us
    pallas_call x9, Pallas kernels, call(): pl.pallas_call(kernel, out_shape=out_shape, in_specs=specs(args, in_hbm,...  7.37 us
    ppermute x10, waiting for transfers between devices, swap(): lax.ppermute(values, axis, [(i, i ^ bit) for i in range(lax.axis_size(axi...  7.02 us
    ppermute x1, starting transfers between devices, branch(): lax.ppermute(sent, ('energy', 'elem'), pairs)  2.65 us
    ppermute x1, waiting for transfers between devices, branch(): lax.ppermute(sent, ('energy', 'elem'), pairs)  2.49 us
  transfers between devices with their start and end apart: 11, of which 7 were waited for; matrix products, arithmetic and copies ran while one was open for 0% of the time, Pallas kernels for 8%

profile of v1, /device:TPU:0, one launch (start us, length us, event | category | flops | bytes accessed | tf_op | source)
XLA Modules:
  0.0 30.2 jit_solution(9866916668615912040)
XLA Ops:
  0.6 1.8 %shard_map.68 = (bf16[2,2,64,128]{3,2,1,0:T(8,128)(2,1)S(1)}, bf16[3,2,64,128]{3,2,1,0:T(8,128)(2,1)S(1)}, bf16[3,2,64,128]{3,2,1,0:T(8,128)(2,1)S(1)}, s32[1]{0...) custom-call(s32[8,4,32]{2,1,0:T(4,128)} %bitcast.3, s32[4,128]{1,0:T(4,128)} %bitcast.4, ...), custom_call_target="tpu_custom_call" | custom-call | flops 16777216 | bytes 536068 | tf_op jit(solution)/shard_map/pallas_call | solution.py:123
  2.4 0.5 %collective-permute-start.45 = (bf16[3,2,64,128]{3,2,1,0:T(8,128)(2,1)S(1)}, bf16[3,2,64,128]{3,2,1,0:T(8,128)(2,1)S(1)}, u32[]{:S(2)}, u32[]{:S(2)}) collective-permute-start(bf16[3,2,64,128]{3,2,1,0:T(8,128)(2,1)S(1)} %get-tuple-element.701), channel_id=1, source_target_pairs={{0,4},{4,0},{8,12},{12,8},{16,20},{20,16},{24,28},{28,24},{1,5},{5... | collective-permute-start | bytes 294920 | tf_op jit(solution)/shard_map/ppermute | solution.py:226
  2.9 0.3 %shard_map.69.picks_ref = bf16[5,128,128]{2,1,0:T(8,128)(2,1)S(1)} custom-call(s32[4,32]{1,0:T(4,128)S(1)} %get-tuple-element.697.rows_ref, s32[2,128]{1,0:T(2,128)S(1)} %get-tuple-element.698.spots_ref), custom_call_target="tpu_custom_call" | custom-call | flops 16777216 | bytes 165376 | tf_op jit(solution)/shard_map/pallas_call | solution.py:123
  3.3 2.6 %collective-permute-start.48 = (bf16[2,2,64,128]{3,2,1,0:T(8,128)(2,1)S(1)}, bf16[2,2,64,128]{3,2,1,0:T(8,128)(2,1)S(1)}, u32[]{:S(2)}, u32[]{:S(2)}) collective-permute-start(bf16[2,2,64,128]{3,2,1,0:T(8,128)(2,1)S(1)} %get-tuple-element.702), channel_id=1, source_target_pairs={{0,16},{4,20},{8,24},{12,28},{16,0},{20,4},{24,8},{28,12},{1,17},{... | collective-permute-start | bytes 196616 | tf_op jit(solution)/shard_map/ppermute | solution.py:226
  5.9 1.9 %collective-permute-start.46 = (bf16[2,2,64,128]{3,2,1,0:T(8,128)(2,1)S(1)}, bf16[2,2,64,128]{3,2,1,0:T(8,128)(2,1)S(1)}, u32[]{:S(2)}, u32[]{:S(2)}) collective-permute-start(bf16[2,2,64,128]{3,2,1,0:T(8,128)(2,1)S(1)} %pad_maximum_fusion), channel_id=1, source_target_pairs={{0,24},{4,28},{8,16},{12,20},{16,8},{20,12},{24,0},{28,4},{1,25},{... | collective-permute-start | bytes 196616 | tf_op jit(solution)/shard_map/ppermute | solution.py:226
  7.8 0.6 %collective-permute-start.47 = (bf16[2,2,64,128]{3,2,1,0:T(8,128)(2,1)S(1)}, bf16[2,2,64,128]{3,2,1,0:T(8,128)(2,1)S(1)}, u32[]{:S(2)}, u32[]{:S(2)}) collective-permute-start(bf16[2,2,64,128]{3,2,1,0:T(8,128)(2,1)S(1)} %pad_maximum_fusion.1), channel_id=1, source_target_pairs={{0,8},{4,12},{8,0},{12,4},{16,24},{20,28},{24,16},{28,20},{1,9},{5... | collective-permute-start | bytes 196616 | tf_op jit(solution)/shard_map/ppermute | solution.py:226
  9.1 2.3 %collective-permute-done.46.diagonal_ref = bf16[2,2,64,128]{3,2,1,0:T(8,128)(2,1)S(1)} collective-permute-done((bf16[2,2,64,128]{3,2,1,0:T(8,128)(2,1)S(1)}, bf16[2,2,64,128]{3,2,1,0:T(8,128)(2,1)S(1)}, u32[]{:S(2)}, u32[]{:S(2)}) %collective-permute-start.46) | collective-permute-done | bytes 65568 | tf_op jit(solution)/shard_map/ppermute | solution.py:226
  11.4 0.7 %collective-permute-done.47.across_ref = bf16[2,2,64,128]{3,2,1,0:T(8,128)(2,1)S(1)} collective-permute-done((bf16[2,2,64,128]{3,2,1,0:T(8,128)(2,1)S(1)}, bf16[2,2,64,128]{3,2,1,0:T(8,128)(2,1)S(1)}, u32[]{:S(2)}, u32[]{:S(2)}) %collective-permute-start.47) | collective-permute-done | bytes 65568 | tf_op jit(solution)/shard_map/ppermute | solution.py:226
  12.1 0.3 shard_map.71
  12.4 7.8 %conditional.1 = (f32[512,256]{1,0:T(8,128)S(1)}, bf16[512,256]{1,0:T(8,128)(2,1)S(1)}, bf16[4,512,512]{2,1,0:T(8,128)(2,1)S(1)}) conditional(s32[]{:T(128)} %bitcast.2, (bf16[512,256]{1,0:T(8,128)(2,1)S(1)}, bf16[5,128,128]{2,1,0:T(8,128)(2,1)S(1)}, bf16[4,512,512]{2,1,0:T(8,128)(2,1)}, ...), branch_computations={%region_0.0_spmd, %region_1.0_spmd, %region_2.0_spmd, %region_3.0_... | conditional | flops 603979776 | bytes 6750272 | solution.py:187
  12.6 2.7 %collective-permute-start.43 = (bf16[512,128]{1,0:T(8,128)(2,1)S(1)}, bf16[512,128]{1,0:T(8,128)(2,1)S(1)}, u32[]{:S(2)}, u32[]{:S(2)}) collective-permute-start(bf16[512,128]{1,0:T(8,128)(2,1)S(1)} %get-tuple-element.666), channel_id=1, source_target_pairs={{0,2},{1,3},{2,0},{3,1},{4,5},{5,4},{6,7},{7,6},{8,11},{9,10},{10,... | collective-permute-start | bytes 393224 | tf_op jit(solution)/shard_map/cond/branch_43_fun/ppermute | solution.py:185
  15.3 2.2 %branch_43_fun.2 = (f32[512,256]{1,0:T(8,128)S(1)}, bf16[512,256]{1,0:T(8,128)(2,1)S(1)}, bf16[4,512,512]{2,1,0:T(8,128)(2,1)S(1)}) custom-call(bf16[512,256]{1,0:T(8,128)(2,1)S(1)} %get-tuple-element.661.signals_ref, bf16[5,128,128]{2,1,0:T(8,128)(2,1)S(1)} %get-tuple-element.662.picks_ref, bf16[4,512,512]{2,1,0:T(8,128)(2,1)} %get-tuple-element.663.table_ref), custom_call_target="tpu_custom_call" | custom-call | flops 536870912 | bytes 5406720 | tf_op jit(solution)/shard_map/cond/branch_43_fun/pallas_call | solution.py:123
  17.5 2.5 %collective-permute-done.43.far_ref = bf16[512,128]{1,0:T(8,128)(2,1)S(1)} collective-permute-done((bf16[512,128]{1,0:T(8,128)(2,1)S(1)}, bf16[512,128]{1,0:T(8,128)(2,1)S(1)}, u32[]{:S(2)}, u32[]{:S(2)}) %collective-permute-start.43) | collective-permute-done | bytes 131104 | tf_op jit(solution)/shard_map/cond/branch_43_fun/ppermute | solution.py:185
  20.0 0.2 branch_43_fun.3
  20.2 1.6 %shard_map.72 = (bf16[2,2,64,128]{3,2,1,0:T(8,128)(2,1)S(1)}, bf16[3,2,64,128]{3,2,1,0:T(8,128)(2,1)S(1)}, bf16[3,2,64,128]{3,2,1,0:T(8,128)(2,1)S(1)}) custom-call(f32[512,256]{1,0:T(8,128)S(1)} %get-tuple-element.705.sums_ref, bf16[512,256]{1,0:T(8,128)(2,1)S(1)} %get-tuple-element.706.partner_ref, bf16[4,512,512]{2,1,0:T(8,128)(2,1)S(1)} %get-tuple-element.707.table_ref), custom_call_target="tpu_custom_call" | custom-call | flops 1073741824 | bytes 3145728 | tf_op jit(solution)/shard_map/pallas_call | solution.py:123
  21.8 0.1 collective-permute-start.50
  21.9 0.8 %collective-permute-start.53 = (bf16[2,2,64,128]{3,2,1,0:T(8,128)(2,1)S(1)}, bf16[2,2,64,128]{3,2,1,0:T(8,128)(2,1)S(1)}, u32[]{:S(2)}, u32[]{:S(2)}) collective-permute-start(bf16[2,2,64,128]{3,2,1,0:T(8,128)(2,1)S(1)} %get-tuple-element.710), channel_id=1, source_target_pairs={{0,16},{4,20},{8,24},{12,28},{16,0},{20,4},{24,8},{28,12},{1,17},{... | collective-permute-start | bytes 196616 | tf_op jit(solution)/shard_map/ppermute | solution.py:226
  22.7 0.5 %collective-permute-done.50.got_ref = bf16[3,2,64,128]{3,2,1,0:T(8,128)(2,1)S(1)} collective-permute-done((bf16[3,2,64,128]{3,2,1,0:T(8,128)(2,1)S(1)}, bf16[3,2,64,128]{3,2,1,0:T(8,128)(2,1)S(1)}, u32[]{:S(2)}, u32[]{:S(2)}) %collective-permute-start.50) | collective-permute-done | bytes 98336 | tf_op jit(solution)/shard_map/ppermute | solution.py:226
  23.2 1.5 %collective-permute-start.51 = (bf16[2,2,64,128]{3,2,1,0:T(8,128)(2,1)S(1)}, bf16[2,2,64,128]{3,2,1,0:T(8,128)(2,1)S(1)}, u32[]{:S(2)}, u32[]{:S(2)}) collective-permute-start(bf16[2,2,64,128]{3,2,1,0:T(8,128)(2,1)S(1)} %pad_maximum_fusion.2), channel_id=1, source_target_pairs={{0,24},{4,28},{8,16},{12,20},{16,8},{20,12},{24,0},{28,4},{1,25},{... | collective-permute-start | bytes 196616 | tf_op jit(solution)/shard_map/ppermute | solution.py:226
  24.7 0.9 %collective-permute-start.52 = (bf16[2,2,64,128]{3,2,1,0:T(8,128)(2,1)S(1)}, bf16[2,2,64,128]{3,2,1,0:T(8,128)(2,1)S(1)}, u32[]{:S(2)}, u32[]{:S(2)}) collective-permute-start(bf16[2,2,64,128]{3,2,1,0:T(8,128)(2,1)S(1)} %pad_maximum_fusion.3), channel_id=1, source_target_pairs={{0,8},{4,12},{8,0},{12,4},{16,24},{20,28},{24,16},{28,20},{1,9},{5... | collective-permute-start | bytes 196616 | tf_op jit(solution)/shard_map/ppermute | solution.py:226
  25.6 0.8 %collective-permute-done.53.refs_1_ = bf16[2,2,64,128]{3,2,1,0:T(8,128)(2,1)S(1)} collective-permute-done((bf16[2,2,64,128]{3,2,1,0:T(8,128)(2,1)S(1)}, bf16[2,2,64,128]{3,2,1,0:T(8,128)(2,1)S(1)}, u32[]{:S(2)}, u32[]{:S(2)}) %collective-permute-start.53) | collective-permute-done | bytes 65568 | tf_op jit(solution)/shard_map/ppermute | solution.py:226
  26.4 2.6 %collective-permute-done.51.diagonal_ref = bf16[2,2,64,128]{3,2,1,0:T(8,128)(2,1)S(1)} collective-permute-done((bf16[2,2,64,128]{3,2,1,0:T(8,128)(2,1)S(1)}, bf16[2,2,64,128]{3,2,1,0:T(8,128)(2,1)S(1)}, u32[]{:S(2)}, u32[]{:S(2)}) %collective-permute-start.51) | collective-permute-done | bytes 65568 | tf_op jit(solution)/shard_map/ppermute | solution.py:226
  29.0 0.2 collective-permute-done.52.across_ref
  29.2 1.0 %shard_map.74 = (bf16[2,64,512]{2,1,0:T(8,128)(2,1)}, bf16[2,64,512]{2,1,0:T(8,128)(2,1)}) custom-call(s32[8,128]{1,0:T(8,128)S(1)} %get-tuple-element.694.lines_ref, bf16[6,2,64,128]{3,2,1,0:T(8,128)(2,1)S(1)} %shard_map.73.refs_0_, bf16[2,2,64,128]{3,2,1,0:T(8,128)(2,1)S(1)} %collective-permute-done.53.refs_1_, ...), custom_call_target="tpu_custom_call" | custom-call | bytes 593920 | tf_op jit(solution)/shard_map/pallas_call | solution.py:123
  (16 shorter events, 0.2 us)
Async XLA Ops:
  2.4 3.4 %collective-permute-start.45 = (bf16[3,2,64,128]{3,2,1,0:T(8,128)(2,1)S(1)}, bf16[3,2,64,128]{3,2,1,0:T(8,128)(2,1)S(1)}, u32[]{:S(2)}, u32[]{:S(2)}) collective-permute-start(bf16[3,2,64,128]{3,2,1,0:T(8,128)(2,1)S(1)} %get-tuple-element.701), channel_id=1, source_target_pairs={{0,4},{4,0},{8,12},{12,8},{16,20},{20,16},{24,28},{28,24},{1,5},{5... | collective-permute-start | bytes 294920 | tf_op jit(solution)/shard_map/ppermute | solution.py:226
  3.3 5.8 %collective-permute-start.48 = (bf16[2,2,64,128]{3,2,1,0:T(8,128)(2,1)S(1)}, bf16[2,2,64,128]{3,2,1,0:T(8,128)(2,1)S(1)}, u32[]{:S(2)}, u32[]{:S(2)}) collective-permute-start(bf16[2,2,64,128]{3,2,1,0:T(8,128)(2,1)S(1)} %get-tuple-element.702), channel_id=1, source_target_pairs={{0,16},{4,20},{8,24},{12,28},{16,0},{20,4},{24,8},{28,12},{1,17},{... | collective-permute-start | bytes 196616 | tf_op jit(solution)/shard_map/ppermute | solution.py:226
  5.9 5.5 %collective-permute-start.46 = (bf16[2,2,64,128]{3,2,1,0:T(8,128)(2,1)S(1)}, bf16[2,2,64,128]{3,2,1,0:T(8,128)(2,1)S(1)}, u32[]{:S(2)}, u32[]{:S(2)}) collective-permute-start(bf16[2,2,64,128]{3,2,1,0:T(8,128)(2,1)S(1)} %pad_maximum_fusion), channel_id=1, source_target_pairs={{0,24},{4,28},{8,16},{12,20},{16,8},{20,12},{24,0},{28,4},{1,25},{... | collective-permute-start | bytes 196616 | tf_op jit(solution)/shard_map/ppermute | solution.py:226
  7.8 4.3 %collective-permute-start.47 = (bf16[2,2,64,128]{3,2,1,0:T(8,128)(2,1)S(1)}, bf16[2,2,64,128]{3,2,1,0:T(8,128)(2,1)S(1)}, u32[]{:S(2)}, u32[]{:S(2)}) collective-permute-start(bf16[2,2,64,128]{3,2,1,0:T(8,128)(2,1)S(1)} %pad_maximum_fusion.1), channel_id=1, source_target_pairs={{0,8},{4,12},{8,0},{12,4},{16,24},{20,28},{24,16},{28,20},{1,9},{5... | collective-permute-start | bytes 196616 | tf_op jit(solution)/shard_map/ppermute | solution.py:226
  9.0 3.1 %collective-permute-start.49 = (bf16[2,2,64,128]{3,2,1,0:T(8,128)(2,1)S(1)}, bf16[2,2,64,128]{3,2,1,0:T(8,128)(2,1)S(1)}, u32[]{:S(2)}, u32[]{:S(2)}) collective-permute-start(bf16[2,2,64,128]{3,2,1,0:T(8,128)(2,1)S(1)} %collective-permute-done.48.refs_1_), channel_id=1, source_target_pairs={{0,4},{4,0},{8,12},{12,8},{16,20},{20,16},{24,28},{28,24},{1,5},{5... | collective-permute-start | bytes 196616 | tf_op jit(solution)/shard_map/ppermute | solution.py:226
  12.6 7.3 %collective-permute-start.43 = (bf16[512,128]{1,0:T(8,128)(2,1)S(1)}, bf16[512,128]{1,0:T(8,128)(2,1)S(1)}, u32[]{:S(2)}, u32[]{:S(2)}) collective-permute-start(bf16[512,128]{1,0:T(8,128)(2,1)S(1)} %get-tuple-element.666), channel_id=1, source_target_pairs={{0,2},{1,3},{2,0},{3,1},{4,5},{5,4},{6,7},{7,6},{8,11},{9,10},{10,... | collective-permute-start | bytes 393224 | tf_op jit(solution)/shard_map/cond/branch_43_fun/ppermute | solution.py:185
  21.8 1.4 %collective-permute-start.50 = (bf16[3,2,64,128]{3,2,1,0:T(8,128)(2,1)S(1)}, bf16[3,2,64,128]{3,2,1,0:T(8,128)(2,1)S(1)}, u32[]{:S(2)}, u32[]{:S(2)}) collective-permute-start(bf16[3,2,64,128]{3,2,1,0:T(8,128)(2,1)S(1)} %get-tuple-element.709), channel_id=1, source_target_pairs={{0,4},{4,0},{8,12},{12,8},{16,20},{20,16},{24,28},{28,24},{1,5},{5... | collective-permute-start | bytes 294920 | tf_op jit(solution)/shard_map/ppermute | solution.py:226
  21.9 4.5 %collective-permute-start.53 = (bf16[2,2,64,128]{3,2,1,0:T(8,128)(2,1)S(1)}, bf16[2,2,64,128]{3,2,1,0:T(8,128)(2,1)S(1)}, u32[]{:S(2)}, u32[]{:S(2)}) collective-permute-start(bf16[2,2,64,128]{3,2,1,0:T(8,128)(2,1)S(1)} %get-tuple-element.710), channel_id=1, source_target_pairs={{0,16},{4,20},{8,24},{12,28},{16,0},{20,4},{24,8},{28,12},{1,17},{... | collective-permute-start | bytes 196616 | tf_op jit(solution)/shard_map/ppermute | solution.py:226
  23.2 5.8 %collective-permute-start.51 = (bf16[2,2,64,128]{3,2,1,0:T(8,128)(2,1)S(1)}, bf16[2,2,64,128]{3,2,1,0:T(8,128)(2,1)S(1)}, u32[]{:S(2)}, u32[]{:S(2)}) collective-permute-start(bf16[2,2,64,128]{3,2,1,0:T(8,128)(2,1)S(1)} %pad_maximum_fusion.2), channel_id=1, source_target_pairs={{0,24},{4,28},{8,16},{12,20},{16,8},{20,12},{24,0},{28,4},{1,25},{... | collective-permute-start | bytes 196616 | tf_op jit(solution)/shard_map/ppermute | solution.py:226
  24.7 4.5 %collective-permute-start.52 = (bf16[2,2,64,128]{3,2,1,0:T(8,128)(2,1)S(1)}, bf16[2,2,64,128]{3,2,1,0:T(8,128)(2,1)S(1)}, u32[]{:S(2)}, u32[]{:S(2)}) collective-permute-start(bf16[2,2,64,128]{3,2,1,0:T(8,128)(2,1)S(1)} %pad_maximum_fusion.3), channel_id=1, source_target_pairs={{0,8},{4,12},{8,0},{12,4},{16,24},{20,28},{24,16},{28,20},{1,9},{5... | collective-permute-start | bytes 196616 | tf_op jit(solution)/shard_map/ppermute | solution.py:226
  26.4 2.8 %collective-permute-start.54 = (bf16[2,2,64,128]{3,2,1,0:T(8,128)(2,1)S(1)}, bf16[2,2,64,128]{3,2,1,0:T(8,128)(2,1)S(1)}, u32[]{:S(2)}, u32[]{:S(2)}) collective-permute-start(bf16[2,2,64,128]{3,2,1,0:T(8,128)(2,1)S(1)} %collective-permute-done.53.refs_1_), channel_id=1, source_target_pairs={{0,4},{4,0},{8,12},{12,8},{16,20},{20,16},{24,28},{28,24},{1,5},{5... | collective-permute-start | bytes 196616 | tf_op jit(solution)/shard_map/ppermute | solution.py:226
